TPU v7x, 256 devices: a whole 4x4x8 slice. The times are simulated.
256 devices in a mesh: task: 16 (over z_lo, y, core), rows: 16 (over z_hi, x).
Axes of the slice: x: 4, y: 4, z: 8 (z_hi: 4, z_lo: 2; z = z_hi * 2 + z_lo), core: 2. Of those that a mesh axis runs over, the one named last changes fastest.
Arguments:
- probes: bfloat16 [16, 384, 8192], P('task', None, 'rows'), may hold values from -48 to 48
- task_weights: bfloat16 [16, 8192, 128], P('task', 'rows'), may hold values from -6 to 6
Outputs:
- merged: float32 [8192, 128], P(('rows', 'task'))
- residual: float32 [8192, 128], P(('rows', 'task'))
All inputs are finite; a program needn't handle non-finite values.
Results may differ from a plain program's by a relative error of at most 0.0003.
Values may be sent and summed in bfloat16 or wider, within the bound.
No kernel may reach another device: no remote copies, remote signals or barrier semaphores. Data moves between devices by JAX's collectives and lax.ppermute only.
A program may use at most 128 MiB of HBM per device.

v0:
```python
import jax
import jax.numpy as jnp
from jax import lax
from jax.sharding import PartitionSpec as P

PROBE = 384
ITERS = 2
ALPHA = 0.9
EPS = 1e-06


def column_squares(vector):
    return lax.psum(jnp.sum(vector * vector, axis=0), ("task", "rows"))


def on_device(probes, task_weights):
    local_x = probes[0]
    local_w = task_weights[0]
    tasks = lax.axis_size("task")
    width = local_x.shape[1]
    share = width // tasks
    cols = local_w.shape[1]
    offset = lax.axis_index("rows") * width
    scale = 1.0 / (PROBE * tasks)
    exact_x = local_x.astype(jnp.float32)
    diag_local = jnp.sum(exact_x * exact_x, axis=0)
    partial_value = jnp.dot(local_x, local_w, preferred_element_type=jnp.float32)
    outputs = lax.psum(partial_value, "rows")
    b_term = ALPHA * jnp.einsum("pd,pc->dc", exact_x, outputs, precision=lax.Precision.HIGHEST)
    b_term = scale * (b_term + (1.0 - ALPHA) * diag_local[:, None] * local_w.astype(jnp.float32))
    raw = jnp.einsum(
        "pd,pe->de",
        local_x,
        lax.all_gather(local_x, "rows", axis=1, tiled=True),
        preferred_element_type=jnp.float32,
    )
    g_term = ALPHA * scale * raw
    square = lax.dynamic_slice_in_dim(g_term, offset, width, 1)
    square = square + jnp.diag((1.0 - ALPHA) * scale * diag_local)
    g_term = lax.dynamic_update_slice_in_dim(g_term, square, offset, 1)
    system, targets = (
        lax.psum_scatter(g_term, "task", scatter_dimension=0, tiled=True),
        lax.psum_scatter(b_term, "task", scatter_dimension=0, tiled=True),
    )
    merged = jnp.zeros((share, cols), jnp.float32)
    residual = targets
    direction = targets
    norm_now = column_squares(residual)
    for step in range(ITERS):
        block = lax.all_gather(direction, "task", axis=0, tiled=True)
        image = jnp.dot(
            system,
            lax.all_gather(block, "rows", axis=0, tiled=True),
            precision=lax.Precision.HIGHEST,
            preferred_element_type=jnp.float32,
        )
        curve = lax.psum(jnp.sum(direction * image, axis=0), ("task", "rows"))
        alpha = norm_now / curve
        merged = merged + alpha * direction
        residual = residual - alpha * image
        norm_next = column_squares(residual)
        direction = residual + norm_next / (norm_now + EPS) * direction
        norm_now = norm_next
    return (merged, residual)


def solution(mesh):
    in_specs = (P("task", None, "rows"), P("task", "rows", None))
    out_specs = (P(("rows", "task"), None), P(("rows", "task"), None))
    return jax.shard_map(
        on_device, mesh=mesh, in_specs=in_specs, out_specs=out_specs, check_vma=False
    )
```

profile of v0, /device:TPU:1, one launch (start us, length us, event | category | flops | bytes accessed | tf_op | source)
XLA Modules:
  0.0 856.5 jit_solution(6923377379118053543)
XLA Ops:
  7.2 0.0 all-reduce.3.cloned.1.call-start
  7.2 2.0 fusion.6
  9.2 0.0 reduce-scatter.7.cloned.1.call-start
  9.2 1.1 multiply_reduce_fusion
  10.4 1.0 copy.11
  11.4 152.3 %all-reduce.3.cloned.1.call-done = f32[384,128]{1,0:T(8,128)} async-done(((f32[384,128]{1,0:T(8,128)}), f32[384,128]{1,0:T(8,128)}) %all-reduce.3.cloned.1.call-update) | async-done | bytes 196624 | tf_op jit(solution)/shard_map/psum | solution.py:28
  163.7 1.5 fusion.3
  165.2 0.8 copy.17
  166.1 0.0 all-gather.9.cloned.1.call-start
  166.1 0.7 all-gather.9.cloned.1.call-update
  166.8 0.0 all-gather.5.cloned.1.call-start
  166.8 68.9 %reduce-scatter.7.cloned.1.call-done = f32[32,128]{1,0:T(8,128)} async-done(((f32[512,128]{1,0:T(8,128)}), f32[32,128]{1,0:T(8,128)}) %reduce-scatter.7.cloned.1.call-update) | async-done | bytes 16400 | tf_op jit(solution)/shard_map/reduce_scatter | solution.py:43
  235.7 22.1 %all_gather.16 = f32[512,128]{1,0:T(8,128)} all-gather(f32[32,128]{1,0:T(8,128)} %reduce-scatter.7.cloned.1.call-done), channel_id=1, replica_groups=mesh['task'=16,'rows'=16] {'task'}, dimensions={0}, use_global_device_ids=true | all-gather | bytes 278528 | tf_op jit(solution)/shard_map/all_gather | solution.py:50
  257.8 0.0 all-gather.5.cloned.1.call-update
  257.9 0.0 reduce-scatter.5.cloned.1.call-start
  257.9 84.4 %all-gather.9.cloned.1.call-done = bf16[1,384,8192]{2,1,0:T(8,128)(2,1)} async-done(((bf16[1,384,512]{2,1,0:T(8,128)(2,1)}), bf16[1,384,8192]{2,1,0:T(8,128)(2,1)}) %all-gather.9.cloned.1.call-update) | async-done | bytes 6291472 | tf_op jit(solution)/shard_map/all_gather | solution.py:34
  342.3 13.2 %convolution_multiply_fusion = f32[512,8192]{1,0:T(8,128)} fusion(bf16[1,384,8192]{2,1,0:T(8,128)(2,1)} %all-gather.9.cloned.1.call-done, bf16[1,384,512]{2,1,0:T(8,128)(2,1)} %param.2), kind=kOutput, calls=%fused_computation | convolution fusion | flops 3225419776 | bytes 23461888 | tf_op jit(solution)/shard_map/pd,pe->de/dot_general | solution.py:31
  355.5 2.4 add_dynamic-update-slice_fusion
  358.0 0.0 all-gather.7.cloned.1.call-start
  358.0 0.6 copy-done.1
  358.7 0.1 copy.18
  358.8 0.1 multiply_reduce_fusion.1
  358.9 59.2 %all-gather.5.cloned.1.call-done = f32[8192,128]{1,0:T(8,128)} async-done(((f32[512,128]{1,0:T(8,128)}), f32[8192,128]{1,0:T(8,128)}) %all-gather.5.cloned.1.call-update) | async-done | bytes 4194320 | tf_op jit(solution)/shard_map/all_gather | solution.py:53
  418.1 102.8 %reduce-scatter.5.cloned.1.call-done = f32[32,8192]{1,0:T(8,128)} async-done(((f32[512,8192]{1,0:T(8,128)}), f32[32,8192]{1,0:T(8,128)}) %reduce-scatter.5.cloned.1.call-update) | async-done | bytes 1048592 | tf_op jit(solution)/shard_map/reduce_scatter | solution.py:42
  520.8 4.9 multiply_reduce_fusion.4
  525.7 77.6 %all-reduce = (f32[128]{0:T(128)S(1)}, f32[128]{0:T(128)S(1)}) all-reduce(f32[128]{0:T(128)S(1)} %multiply_reduce_fusion.1, f32[128]{0:T(128)S(1)} %get-tuple-element.10), channel_id=1, replica_groups=mesh['task'=16,'rows'=16] {'task','rows'}, use_global_device_ids=true, to_apply=%region_4.5 | all-reduce | flops 256 | bytes 2048 | tf_op jit(solution)/shard_map/psum | solution.py:13
  603.4 73.2 %psum.38 = f32[128]{0:T(128)S(1)} all-reduce(f32[128]{0:T(128)S(1)} %multiply_reduce_fusion.3), channel_id=1, replica_groups=mesh['task'=16,'rows'=16] {'task','rows'}, use_global_device_ids=true, to_apply=%region_9.10 | all-reduce | flops 128 | bytes 1024 | tf_op jit(solution)/shard_map/psum | solution.py:13
  676.5 21.1 %all_gather.18 = f32[512,128]{1,0:T(8,128)} all-gather(f32[32,128]{1,0:T(8,128)S(1)} %multiply_add_fusion.1), channel_id=1, replica_groups=mesh['task'=16,'rows'=16] {'task'}, dimensions={0}, use_global_device_ids=true | all-gather | bytes 278528 | tf_op jit(solution)/shard_map/all_gather | solution.py:50
  697.7 68.8 %all-gather.7.cloned.1.call-done = f32[8192,128]{1,0:T(8,128)} async-done(((f32[512,128]{1,0:T(8,128)}), f32[8192,128]{1,0:T(8,128)}) %all-gather.7.cloned.1.call-update) | async-done | bytes 4194320 | tf_op jit(solution)/shard_map/all_gather | solution.py:53
  766.5 4.0 multiply_reduce_fusion.2
  770.5 78.4 %psum.39 = f32[128]{0:T(128)S(1)} all-reduce(f32[128]{0:T(128)S(1)} %get-tuple-element.12), channel_id=1, replica_groups=mesh['task'=16,'rows'=16] {'task','rows'}, use_global_device_ids=true, to_apply=%region_11.12 | all-reduce | flops 128 | bytes 1024 | tf_op jit(solution)/shard_map/psum | solution.py:57
  849.0 0.6 multiply_subtract_fusion
  (13 shorter events, 0.1 us)
Async XLA Ops:
  7.2 156.5 %all-reduce.3.cloned.1.call-start = ((), (), s32[]{:S(2)}) async-start(), calls=%async_computation.2 | async-start | bytes 393216 | tf_op jit(solution)/shard_map/psum | solution.py:28
  9.2 226.5 %reduce-scatter.7.cloned.1.call-start = ((), (), s32[]{:S(2)}) async-start(), calls=%async_computation.7 | async-start | bytes 278528 | tf_op jit(solution)/shard_map/reduce_scatter | solution.py:43
  166.1 176.3 %all-gather.9.cloned.1.call-start = ((), (), s32[]{:S(2)}) async-start(), calls=%async_computation.6 | async-start | bytes 6684672 | tf_op jit(solution)/shard_map/all_gather | solution.py:34
  166.8 251.3 %all-gather.5.cloned.1.call-start = ((), (), s32[]{:S(2)}) async-start(), calls=%async_computation.4 | async-start | bytes 4456448 | tf_op jit(solution)/shard_map/all_gather | solution.py:53
  257.9 263.0 %reduce-scatter.5.cloned.1.call-start = ((), (), s32[]{:S(2)}) async-start(), calls=%async_computation.3 | async-start | bytes 17825792 | tf_op jit(solution)/shard_map/reduce_scatter | solution.py:42
  357.9 0.7 copy-start.1
  358.0 408.5 %all-gather.7.cloned.1.call-start = ((), (), s32[]{:S(2)}) async-start(), calls=%async_computation.5 | async-start | bytes 4456448 | tf_op jit(solution)/shard_map/all_gather | solution.py:53
  520.8 245.6 %copy-start = (f32[32,8192]{1,0:T(8,128)S(1)}, f32[32,8192]{1,0:T(8,128)}, u32[]{:S(2)}) copy-start(f32[32,8192]{1,0:T(8,128)} %reduce-scatter.5.cloned.1.call-done) | copy-start | bytes 3145732
Sparse Core Ops, SparseCore 0:
  10.6 153.0 all-reduce.2
  166.2 69.4 reduce-scatter.6
  238.1 104.1 all-gather.8
  344.6 73.4 all-gather.4
  420.5 100.3 reduce-scatter.4
  697.8 68.6 all-gather.6
where the time goes:
time: 857 us; the launch traced here: 856 us
  waiting for transfers between devices  537 us (63%)
  blocking collectives  272 us (32%)
  matrix products  25.6 us (3%)
  between operations  14.2 us (2%)
    psum x1, waiting for transfers between devices, on_device(): outputs = lax.psum(partial_value, 'rows')  152 us
    psum x2, blocking collectives, column_squares(): return lax.psum(jnp.sum(vector * vector, axis=0), ('task', 'rows'))  151 us
    all_gather x2, waiting for transfers between devices, on_device(): lax.all_gather(block, 'rows', axis=0, tiled=True)  128 us
    reduce_scatter x1, waiting for transfers between devices, on_device(): lax.psum_scatter(g_term, 'task', scatter_dimension=0, tiled=True)  103 us
    all_gather x1, waiting for transfers between devices, on_device(): lax.all_gather(local_x, 'rows', axis=1, tiled=True)  84.4 us
    psum x1, blocking collectives, on_device(): curve = lax.psum(jnp.sum(direction * image, axis=0), ('task', 'rows'))  78.4 us
    reduce_scatter x1, waiting for transfers between devices, on_device(): lax.psum_scatter(b_term, 'task', scatter_dimension=0, tiled=True)  68.9 us
    all_gather x2, blocking collectives, on_device(): block = lax.all_gather(direction, 'task', axis=0, tiled=True)  43.2 us
  transfers between devices with their start and end apart: 6, of which 6 were waited for; matrix products, arithmetic and copies ran while one was open for 2% of the time, Pallas kernels for 0%

commit v1 on v0

--- a/solution.py
+++ b/solution.py
@@ -25,7 +25,8 @@
     exact_x = local_x.astype(jnp.float32)
     diag_local = jnp.sum(exact_x * exact_x, axis=0)
     partial_value = jnp.dot(local_x, local_w, preferred_element_type=jnp.float32)
-    outputs = lax.psum(partial_value, "rows")
+    terms = lax.all_gather(partial_value, "rows", axis=0, tiled=False)
+    outputs = terms.sum(axis=0)
     b_term = ALPHA * jnp.einsum("pd,pc->dc", exact_x, outputs, precision=lax.Precision.HIGHEST)
     b_term = scale * (b_term + (1.0 - ALPHA) * diag_local[:, None] * local_w.astype(jnp.float32))
     raw = jnp.einsum(

time: 857 us -> 766 us (0.89)
  waiting for transfers between devices: 537 us -> 447 us
    psum x1 -> x0, waiting for transfers between devices: 152 us -> none  [on_device(): outputs = lax.psum(partial_value, 'rows')]
    all_gather x0 -> x1, waiting for transfers between devices: none -> 70.1 us  [on_device(): terms = lax.all_gather(partial_value, 'rows', axis=0, tiled=False)]
    reduce_scatter x1, waiting for transfers between devices: 68.9 us -> 58.1 us  [on_device(): lax.psum_scatter(b_term, 'task', scatter_dimension=0, tiled=True)]
where the time goes in v1:
time: 766 us
  waiting for transfers between devices  447 us (58%)
  blocking collectives  272 us (36%)
  matrix products  23.2 us (3%)
  between operations  14.2 us (2%)
    psum x2, blocking collectives, column_squares(): return lax.psum(jnp.sum(vector * vector, axis=0), ('task', 'rows'))  151 us
    all_gather x2, waiting for transfers between devices, on_device(): lax.all_gather(block, 'rows', axis=0, tiled=True)  130 us
    reduce_scatter x1, waiting for transfers between devices, on_device(): lax.psum_scatter(g_term, 'task', scatter_dimension=0, tiled=True)  103 us
    all_gather x1, waiting for transfers between devices, on_device(): lax.all_gather(local_x, 'rows', axis=1, tiled=True)  84.6 us
    psum x1, blocking collectives, on_device(): curve = lax.psum(jnp.sum(direction * image, axis=0), ('task', 'rows'))  78.5 us
    all_gather x1, waiting for transfers between devices, on_device(): terms = lax.all_gather(partial_value, 'rows', axis=0, tiled=False)  70.1 us
    reduce_scatter x1, waiting for transfers between devices, on_device(): lax.psum_scatter(b_term, 'task', scatter_dimension=0, tiled=True)  58.1 us
    all_gather x2, blocking collectives, on_device(): block = lax.all_gather(direction, 'task', axis=0, tiled=True)  43.2 us
  transfers between devices with their start and end apart: 6, of which 6 were waited for; matrix products, arithmetic and copies ran while one was open for 2% of the time, Pallas kernels for 0%

profile of v1, /device:TPU:1, one launch (start us, length us, event | category | flops | bytes accessed | tf_op | source)
XLA Modules:
  0.0 765.7 jit_solution(10110276740427094737)
XLA Ops:
  7.2 0.0 all-gather.11.cloned.1.call-start
  7.2 2.0 fusion.6
  9.3 0.0 reduce-scatter.7.cloned.1.call-start
  9.3 1.0 copy.11
  10.3 1.1 multiply_reduce_fusion
  11.4 70.1 %all-gather.11.cloned.1.call-done = f32[6144,128]{1,0:T(8,128)} async-done(((f32[384,128]{1,0:T(8,128)}), f32[6144,128]{1,0:T(8,128)}) %all-gather.11.cloned.1.call-update) | async-done | bytes 3145744 | tf_op jit(solution)/shard_map/all_gather | solution.py:28
  81.5 2.1 reduce_sum.54
  83.6 1.4 fusion.3
  85.0 0.8 copy.17
  85.9 0.0 all-gather.13.cloned.1.call-start
  85.9 0.7 all-gather.13.cloned.1.call-update
  86.6 0.0 all-gather.7.cloned.1.call-start
  86.6 58.1 %reduce-scatter.7.cloned.1.call-done = f32[32,128]{1,0:T(8,128)} async-done(((f32[512,128]{1,0:T(8,128)}), f32[32,128]{1,0:T(8,128)}) %reduce-scatter.7.cloned.1.call-update) | async-done | bytes 16400 | tf_op jit(solution)/shard_map/reduce_scatter | solution.py:44
  144.7 22.1 %all_gather.24 = f32[512,128]{1,0:T(8,128)} all-gather(f32[32,128]{1,0:T(8,128)} %reduce-scatter.7.cloned.1.call-done), channel_id=1, replica_groups=mesh['task'=16,'rows'=16] {'task'}, dimensions={0}, use_global_device_ids=true | all-gather | bytes 278528 | tf_op jit(solution)/shard_map/all_gather | solution.py:51
  166.9 0.0 reduce-scatter.5.cloned.1.call-start
  166.9 84.6 %all-gather.13.cloned.1.call-done = bf16[1,384,8192]{2,1,0:T(8,128)(2,1)} async-done(((bf16[1,384,512]{2,1,0:T(8,128)(2,1)}), bf16[1,384,8192]{2,1,0:T(8,128)(2,1)}) %all-gather.13.cloned.1.call-update) | async-done | bytes 6291472 | tf_op jit(solution)/shard_map/all_gather | solution.py:35
  251.5 10.9 %convolution_multiply_fusion = f32[512,8192]{1,0:T(8,128)} fusion(bf16[1,384,8192]{2,1,0:T(8,128)(2,1)} %all-gather.13.cloned.1.call-done, bf16[1,384,512]{2,1,0:T(8,128)(2,1)S(1)} %copy-done), kind=kOutput, calls=%fused_computation | convolution fusion | flops 3225419776 | bytes 23461888 | tf_op jit(solution)/shard_map/pd,pe->de/dot_general | solution.py:32
  262.4 2.4 add_dynamic-update-slice_fusion
  264.8 0.0 all-gather.9.cloned.1.call-start
  264.9 0.6 copy-done.2
  265.5 0.1 copy.18
  265.6 0.1 multiply_reduce_fusion.1
  265.7 61.6 %all-gather.7.cloned.1.call-done = f32[8192,128]{1,0:T(8,128)} async-done(((f32[512,128]{1,0:T(8,128)}), f32[8192,128]{1,0:T(8,128)}) %all-gather.7.cloned.1.call-update) | async-done | bytes 4194320 | tf_op jit(solution)/shard_map/all_gather | solution.py:54
  327.3 102.8 %reduce-scatter.5.cloned.1.call-done = f32[32,8192]{1,0:T(8,128)} async-done(((f32[512,8192]{1,0:T(8,128)}), f32[32,8192]{1,0:T(8,128)}) %reduce-scatter.5.cloned.1.call-update) | async-done | bytes 1048592 | tf_op jit(solution)/shard_map/reduce_scatter | solution.py:43
  430.1 4.9 multiply_reduce_fusion.4
  434.9 77.6 %all-reduce = (f32[128]{0:T(128)S(1)}, f32[128]{0:T(128)S(1)}) all-reduce(f32[128]{0:T(128)S(1)} %multiply_reduce_fusion.1, f32[128]{0:T(128)S(1)} %get-tuple-element.10), channel_id=1, replica_groups=mesh['task'=16,'rows'=16] {'task','rows'}, use_global_device_ids=true, to_apply=%region_4.5 | all-reduce | flops 256 | bytes 2048 | tf_op jit(solution)/shard_map/psum | solution.py:13
  512.6 73.2 %psum.30 = f32[128]{0:T(128)S(1)} all-reduce(f32[128]{0:T(128)S(1)} %multiply_reduce_fusion.3), channel_id=1, replica_groups=mesh['task'=16,'rows'=16] {'task','rows'}, use_global_device_ids=true, to_apply=%region_9.10 | all-reduce | flops 128 | bytes 1024 | tf_op jit(solution)/shard_map/psum | solution.py:13
  585.8 21.1 %all_gather.26 = f32[512,128]{1,0:T(8,128)} all-gather(f32[32,128]{1,0:T(8,128)S(1)} %multiply_add_fusion.1), channel_id=1, replica_groups=mesh['task'=16,'rows'=16] {'task'}, dimensions={0}, use_global_device_ids=true | all-gather | bytes 278528 | tf_op jit(solution)/shard_map/all_gather | solution.py:51
  606.9 68.8 %all-gather.9.cloned.1.call-done = f32[8192,128]{1,0:T(8,128)} async-done(((f32[512,128]{1,0:T(8,128)}), f32[8192,128]{1,0:T(8,128)}) %all-gather.9.cloned.1.call-update) | async-done | bytes 4194320 | tf_op jit(solution)/shard_map/all_gather | solution.py:54
  675.7 4.0 multiply_reduce_fusion.2
  679.8 78.5 %psum.31 = f32[128]{0:T(128)S(1)} all-reduce(f32[128]{0:T(128)S(1)} %get-tuple-element.12), channel_id=1, replica_groups=mesh['task'=16,'rows'=16] {'task','rows'}, use_global_device_ids=true, to_apply=%region_11.12 | all-reduce | flops 128 | bytes 1024 | tf_op jit(solution)/shard_map/psum | solution.py:58
  758.2 0.6 multiply_subtract_fusion
  (16 shorter events, 0.1 us)
Async XLA Ops:
  7.2 244.4 %copy-start = (bf16[1,384,512]{2,1,0:T(8,128)(2,1)S(1)}, bf16[1,384,512]{2,1,0:T(8,128)(2,1)}, u32[]{:S(2)}) copy-start(bf16[1,384,512]{2,1,0:T(8,128)(2,1)} %param.2) | copy-start | bytes 1179652
  7.2 74.3 %all-gather.11.cloned.1.call-start = ((), (), s32[]{:S(2)}) async-start(), calls=%async_computation.5 | async-start | bytes 3342336 | tf_op jit(solution)/shard_map/all_gather | solution.py:28
  9.3 135.5 %reduce-scatter.7.cloned.1.call-start = ((), (), s32[]{:S(2)}) async-start(), calls=%async_computation.7 | async-start | bytes 278528 | tf_op jit(solution)/shard_map/reduce_scatter | solution.py:44
  85.9 165.7 %all-gather.13.cloned.1.call-start = ((), (), s32[]{:S(2)}) async-start(), calls=%async_computation.6 | async-start | bytes 6684672 | tf_op jit(solution)/shard_map/all_gather | solution.py:35
  86.6 240.7 %all-gather.7.cloned.1.call-start = ((), (), s32[]{:S(2)}) async-start(), calls=%async_computation.3 | async-start | bytes 4456448 | tf_op jit(solution)/shard_map/all_gather | solution.py:54
  166.9 263.2 %reduce-scatter.5.cloned.1.call-start = ((), (), s32[]{:S(2)}) async-start(), calls=%async_computation.2 | async-start | bytes 17825792 | tf_op jit(solution)/shard_map/reduce_scatter | solution.py:43
  264.8 0.7 copy-start.2
  264.8 410.9 %all-gather.9.cloned.1.call-start = ((), (), s32[]{:S(2)}) async-start(), calls=%async_computation.4 | async-start | bytes 4456448 | tf_op jit(solution)/shard_map/all_gather | solution.py:54
  430.1 245.7 %copy-start.1 = (f32[32,8192]{1,0:T(8,128)S(1)}, f32[32,8192]{1,0:T(8,128)}, u32[]{:S(2)}) copy-start(f32[32,8192]{1,0:T(8,128)} %reduce-scatter.5.cloned.1.call-done) | copy-start | bytes 3145732
Sparse Core Ops, SparseCore 0:
  10.4 71.0 all-gather.10
  86.0 58.7 reduce-scatter.6
  147.1 104.3 all-gather.12
  253.8 73.4 all-gather.6
  329.7 100.3 reduce-scatter.4
  607.0 68.6 all-gather.8
